TPU v7x, 32 devices: a whole 2x2x4 slice. The times are simulated.
32 devices in a mesh: panel: 8 (over z, y), obs: 4 (over x, core).
Axes of the slice: x: 2, y: 2, z: 4, core: 2. Of those that a mesh axis runs over, the one named last changes fastest.
Arguments:
- flow_blocks: bfloat16 [1024, 4, 1280], P('panel'), may hold values from -6 to 6
- interp_weights: bfloat16 [32, 128, 512], P(('panel', 'obs')), may hold values from -0.25 to 0.25
- donor_owner: int32 [4096, 1], P(('panel', 'obs')), may hold values from 0 to 7; in each aligned block of 128 rows (0 to 127, 128 to 255, ...) at most 24 rows name the same one
- donor_block: int32 [4096], P(('panel', 'obs')), may hold values from 0 to 127
- panel_normals: float32 [3, 4096], P(None, ('panel', 'obs')), may hold values from -3 to 3
- panel_points: float32 [3, 4096], P(None, ('panel', 'obs')), may hold values from -1 to 1
- observer_points: float32 [3, 1024], P(None, 'obs'), may hold values from -12 to 12, as said below
Outputs:
- pressure: float32 [128, 1024], P('panel', 'obs')
Inputs may be any that keep to these rules, and one draw needn't show every extreme that they name: `donor_owner`: within the rows of one device, no owner index is named by more than 24 rows; some devices' rows name one owner exactly 24 times. `observer_points`: every observer lies between 6 and 12 from the anchor.
All inputs are finite; a program needn't handle non-finite values.
Results may differ from a plain program's by a relative error of at most 0.0003.
Values may be sent and summed in bfloat16 or wider, within the bound.
A program may use at most 64 MiB of HBM per device.

v0:
```python
import math

import jax
import jax.numpy as jnp
from jax import lax
from jax.sharding import PartitionSpec as P

NV = 5
NT = 256
HARM = 64


KAPPA = 0.5


def fourier_table(samples, orders):
    sample_ids = jnp.arange(samples, dtype=jnp.int32)
    harmonic = jnp.arange(1, orders + 1, dtype=jnp.int32)
    wrapped = sample_ids[:, None] * harmonic[None, :] % samples
    angles = wrapped.astype(jnp.float32) * (2.0 * math.pi / samples)
    factor = 2.0 / samples
    return jnp.concatenate([factor * jnp.cos(angles), -factor * jnp.sin(angles)], axis=1)


def spectra_of(values, normals, transform, samples):
    panels = values.shape[0]
    fields = values.reshape(panels, NV, samples)
    density = 1.0 + fields[:, 0]
    velocity = fields[:, 1:4]
    pressure_pert = fields[:, 4]
    normal_vec = jnp.transpose(normals)[:, :, None]
    normal_flow = jnp.sum(velocity * normal_vec, axis=1)
    mass_flux = density * normal_flow
    loading = pressure_pert[:, None, :] * normal_vec + mass_flux[:, None, :] * velocity
    series = jnp.concatenate([mass_flux[:, None, :], loading], axis=1)
    return jnp.einsum("pct,tk->ckp", series, transform, precision=lax.Precision.HIGHEST)


def doubled(base_phase, orders):
    cosines = jnp.cos(base_phase)[None]
    sines = jnp.sin(base_phase)[None]
    while cosines.shape[0] < orders:
        last_cos = cosines[-1]
        last_sin = sines[-1]
        cosines, sines = (
            jnp.concatenate([cosines, cosines * last_cos - sines * last_sin], axis=0),
            jnp.concatenate([sines, sines * last_cos + cosines * last_sin], axis=0),
        )
    return (cosines, sines)


def radiate(spectra, points, observers):
    orders = spectra.shape[1] // 2
    offset_vec = observers[:, None, :] - points[:, :, None]
    distance = jnp.sqrt(jnp.sum(offset_vec * offset_vec, axis=0))
    inverse = 1.0 / distance
    direction = offset_vec * inverse[None]
    wavenum = (KAPPA * jnp.arange(1, orders + 1, dtype=jnp.float32))[:, None, None]
    load_re = (
        spectra[1, :orders][:, :, None] * direction[0][None]
        + spectra[2, :orders][:, :, None] * direction[1][None]
        + spectra[3, :orders][:, :, None] * direction[2][None]
    )
    load_im = (
        spectra[1, orders:][:, :, None] * direction[0][None]
        + spectra[2, orders:][:, :, None] * direction[1][None]
        + spectra[3, orders:][:, :, None] * direction[2][None]
    )
    amp_re = load_re * inverse[None] - wavenum * (spectra[0, orders:][:, :, None] + load_im)
    amp_im = load_im * inverse[None] + wavenum * (spectra[0, :orders][:, :, None] + load_re)
    cosines, sines = doubled(KAPPA * distance, orders)
    spreading = (inverse / (4.0 * math.pi))[None]
    real_part = jnp.sum((amp_re * cosines + amp_im * sines) * spreading, axis=1)
    imag_part = jnp.sum((amp_im * cosines - amp_re * sines) * spreading, axis=1)
    return jnp.concatenate([real_part, imag_part], axis=0)


def radiate_all(spectra, points, observers):
    panel_total = spectra.shape[1]
    block_size = math.gcd(panel_total, max(1, 32768 // observers.shape[1]))
    block_count = panel_total // block_size

    def one_block(block_index, running):
        first_panel = block_index * block_size
        block_spectra = lax.dynamic_slice_in_dim(spectra, first_panel, block_size, 1)
        block_points = lax.dynamic_slice_in_dim(points, first_panel, block_size, 1)
        return running + radiate(block_spectra.reshape(4, -1, block_size), block_points, observers)

    initial = jnp.zeros((spectra.shape[0] // 4, observers.shape[1]), jnp.float32)
    return lax.fori_loop(0, block_count, one_block, initial)


def body(
    flow_blocks,
    interp_weights,
    donor_owner,
    donor_block,
    panel_normals,
    panel_points,
    observer_points,
):
    peer_count = lax.axis_size("panel")
    tile_count, tile_width, stencil = interp_weights.shape
    cell_count = flow_blocks.shape[1]
    slot_count = stencil // cell_count
    row_count = tile_count * slot_count
    capacity = max(2, (3 * row_count + 2 * peer_count - 1) // (2 * peer_count))
    owner_of = donor_owner[:, 0]
    matches = (owner_of[:, None] == jnp.arange(peer_count, dtype=jnp.int32)[None, :]).astype(
        jnp.int32
    )
    slot_rank = jnp.sum(jnp.cumsum(matches, axis=0) * matches, axis=1) - 1
    requests = jnp.zeros((peer_count, capacity), jnp.int32).at[owner_of, slot_rank].set(donor_block)
    found = jnp.take(
        flow_blocks,
        lax.all_to_all(requests, "panel", split_axis=0, concat_axis=0, tiled=True),
        axis=0,
    )
    arrived = lax.all_to_all(found, "panel", split_axis=0, concat_axis=0, tiled=True)
    history = arrived.shape[-1]
    flat_rows = arrived.reshape(peer_count * capacity, cell_count, history)
    picked = jnp.take(flat_rows, owner_of * capacity + slot_rank, axis=0)
    donors = picked.reshape(tile_count, stencil, history)
    values = jnp.einsum("tpc,tcv->tpv", interp_weights, donors, preferred_element_type=jnp.float32)
    values = values.reshape(tile_count * tile_width, history)
    transform = fourier_table(NT, HARM)
    spectra = spectra_of(values, panel_normals, transform, NT).reshape(8 * HARM, -1)
    group_spectra, group_points = (
        lax.all_gather(spectra, "obs", axis=1, tiled=True),
        lax.all_gather(panel_points, "obs", axis=1, tiled=True),
    )
    partial_sum = radiate_all(group_spectra, group_points, observer_points)
    pressure = lax.psum_scatter(partial_sum, "panel", scatter_dimension=0, tiled=True)
    return pressure


def solution(mesh):
    return jax.shard_map(
        body,
        mesh=mesh,
        in_specs=(
            P("panel", None, None),
            P(("panel", "obs"), None, None),
            P(("panel", "obs"), None),
            P(("panel", "obs")),
            P(None, ("panel", "obs")),
            P(None, ("panel", "obs")),
            P(None, "obs"),
        ),
        out_specs=P("panel", "obs"),
        check_vma=False,
    )
```

profile of v0, /device:TPU:0, one launch (start us, length us, event | category | flops | bytes accessed | tf_op | source)
XLA Modules:
  0.0 293.3 jit_solution(16103887180533172883)
XLA Ops:
  6.5 0.8 fusion.25
  7.6 0.8 select_reduce_fusion
  8.4 0.7 fusion.30
  9.1 11.0 %scatter_fusion = s32[8,24]{1,0:T(8,128)S(1)} fusion(s32[8,24]{1,0:T(8,128)S(1)} %broadcast_in_dim.61, s32[128]{0:T(128)S(1)} %fusion.30, s32[128]{0:T(128)} %param.12), kind=kCustom, calls=%fused_computation.2 | custom fusion | bytes 2560 | tf_op jit(solution)/shard_map/scatter | solution.py:113
  20.0 13.6 %all_to_all.20 = s32[8,1,24]{2,1,0:T(1,128)S(1)} all-to-all(s32[8,1,24]{2,1,0:T(1,128)S(1)} %bitcast.163), channel_id=1, replica_groups=mesh['panel'=8,'obs'=4] {'panel'}, dimensions={0} | all-to-all | bytes 1536 | tf_op jit(solution)/shard_map/all_to_all | solution.py:116
  33.8 2.3 gather_fusion
  36.1 2.1 broadcast_select_fusion
  38.2 3.6 %all-to-all-start.1 = ((bf16[8,24,4,1280]{3,2,1,0:T(4,128)(2,1)}), bf16[8,24,4,1280]{3,2,1,0:T(4,128)(2,1)S(1)}, u32[]{:S(2)}, u32[]{:S(2)}) async-start(bf16[8,24,4,1280]{3,2,1,0:T(4,128)(2,1)} %broadcast_select_fusion), calls=%async_computation.1 | async-start | bytes 3932160 | tf_op jit(solution)/shard_map/all_to_all | solution.py:119
  42.3 43.7 %all-to-all-done.1 = bf16[8,24,4,1280]{3,2,1,0:T(4,128)(2,1)S(1)} async-done(((bf16[8,24,4,1280]{3,2,1,0:T(4,128)(2,1)}), bf16[8,24,4,1280]{3,2,1,0:T(4,128)(2,1)S(1)}, u32[]{:S(2)}, u32[]{:S(2)}) %all-to-all-start.1) | async-done | bytes 1966112 | tf_op jit(solution)/shard_map/all_to_all | solution.py:119
  86.0 2.7 gather_fusion.1
  88.7 2.0 broadcast_select_fusion.1
  90.7 1.3 select_n.80
  92.0 1.9 fusion.20
  94.6 1.3 fusion.14
  96.0 5.4 %all_gather.7 = f32[3,512]{1,0:T(4,128)S(1)} all-gather(f32[3,128]{1,0:T(4,128)S(1)} %copy-done.8), channel_id=1, replica_groups=mesh['panel'=8,'obs'=4] {'obs'}, dimensions={1}, use_global_device_ids=true | all-gather | bytes 7680 | tf_op jit(solution)/shard_map/all_gather | solution.py:130
  101.4 10.6 %all-gather.2.cloned.1.call-done = f32[512,512]{1,0:T(8,128)} async-done(((f32[512,128]{1,0:T(8,128)}), f32[512,512]{1,0:T(8,128)}) %all-gather.2.cloned.1.call-update) | async-done | bytes 1048592 | tf_op jit(solution)/shard_map/all_gather | solution.py:129
  112.0 111.8 %while.14 = (s32[]{:T(128)}, f32[128,256]{1,0:T(8,128)}, f32[512,512]{1,0:T(8,128)}, f32[3,256]{1,0:T(4,128)S(1)}, f32[3,512]{1,0:T(4,128)S(1)}, /*index=5*/s32[]{:T(128)}, s32[]{:T(128)}, s32[]{:T(128)}, s32[]{:T(128)}) while((s32[]{:T(128)}, f32[128,256]{1,0:T(8,128)}, f32[512,512]{1,0:T(8,128)}, f32[3,256]{1,0:T(4,128)S(1)}, ...), condition=%wide.region_8.9_spmd.clone, body=%wide.region_4.8_spmd.clone.sunk | while | flops 76873856 | bytes 116667128 | solution.py:90
  112.6 0.5 fusion.41
  113.1 0.5 fusion.43
  113.7 0.5 fusion.42
  115.6 1.8 copy-done.1
  117.3 0.7 copy-done.2
  118.0 3.5 %constant_dynamic-update-slice_fusion.42 = (f32[64,128,256]{2,1,0:T(8,128)S(1)}, f32[16,128,256]{2,1,0:T(8,128)S(1)}, f32[32,128,256]{2,1,0:T(8,128)}, f32[16,128,256]{2,1,0:T(8,128)S(1)}) fusion(f32[64,128,256]{2,1,0:T(8,128)S(1)} %get-tuple-element.325, f32[16,128,256]{2,1,0:T(8,128)} %copy-done.2, f32[128,256]{1,0:T(8,128)S(1)} %slice_bitcast_fusion.32, ...), kind=kLoop, calls=%fused_computation.74.clone.1 | loop fusion | flops 3145728 | bytes 12845056 | tf_op jit(solution)/shard_map/while
  121.9 0.7 slice_bitcast_fusion.34
  122.6 0.7 slice_bitcast_fusion.35
  123.3 4.2 %subtract_dynamic-update-slice_fusion.2 = (f32[64,128,256]{2,1,0:T(8,128)S(1)}, f32[64,128,256]{2,1,0:T(8,128)S(1)}) fusion(f32[64,128,256]{2,1,0:T(8,128)S(1)} %get-tuple-element.343, f32[32,128,256]{2,1,0:T(8,128)} %get-tuple-element.344, f32[32,128,256]{2,1,0:T(8,128)S(1)} %constant_dynamic-update-slice_fusion.43, ...), kind=kLoop, calls=%fused_computation.10.clone.1 | loop fusion | flops 6291456 | bytes 17039360 | tf_op jit(solution)/shard_map/while/body/eval_jaxpr/concatenate | solution.py:46
  127.6 1.0 constant_dynamic-slice_fusion.5
  128.6 10.6 %multiply_reduce_fusion.4 = (f32[64,256]{1,0:T(8,128)S(1)}, f32[64,256]{1,0:T(8,128)S(1)}) fusion(f32[64,128,256]{2,1,0:T(8,128)S(1)} %get-tuple-element.349, f32[64,128,256]{2,1,0:T(8,128)S(1)} %get-tuple-element.350, f32[128,256]{1,0:T(8,128)S(1)} %get-tuple-element.351, f32[64,128]{1,0:T(8,128)S(1)} %get-tuple-element.352, ...), kind=kLoop, calls=%fused_computation.4.clone.1 | loop fusion | flops 58687488 | bytes 17826048 | tf_op jit(solution)/shard_map/while/body/eval_jaxpr/reduce_sum | solution.py:73
  139.3 0.6 copy-done.4
  140.5 0.5 fusion.41
  141.6 0.5 fusion.42
  143.5 1.8 copy-done.1
  145.3 0.7 copy-done.2
  146.0 3.5 %constant_dynamic-update-slice_fusion.42 = (f32[64,128,256]{2,1,0:T(8,128)S(1)}, f32[16,128,256]{2,1,0:T(8,128)S(1)}, f32[32,128,256]{2,1,0:T(8,128)}, f32[16,128,256]{2,1,0:T(8,128)S(1)}) fusion(f32[64,128,256]{2,1,0:T(8,128)S(1)} %get-tuple-element.325, f32[16,128,256]{2,1,0:T(8,128)} %copy-done.2, f32[128,256]{1,0:T(8,128)S(1)} %slice_bitcast_fusion.32, ...), kind=kLoop, calls=%fused_computation.74.clone.1 | loop fusion | flops 3145728 | bytes 12845056 | tf_op jit(solution)/shard_map/while
  149.9 0.7 slice_bitcast_fusion.34
  150.5 0.7 slice_bitcast_fusion.35
  151.2 4.2 %subtract_dynamic-update-slice_fusion.2 = (f32[64,128,256]{2,1,0:T(8,128)S(1)}, f32[64,128,256]{2,1,0:T(8,128)S(1)}) fusion(f32[64,128,256]{2,1,0:T(8,128)S(1)} %get-tuple-element.343, f32[32,128,256]{2,1,0:T(8,128)} %get-tuple-element.344, f32[32,128,256]{2,1,0:T(8,128)S(1)} %constant_dynamic-update-slice_fusion.43, ...), kind=kLoop, calls=%fused_computation.10.clone.1 | loop fusion | flops 6291456 | bytes 17039360 | tf_op jit(solution)/shard_map/while/body/eval_jaxpr/concatenate | solution.py:46
  155.5 1.0 constant_dynamic-slice_fusion.5
  156.6 10.6 %multiply_reduce_fusion.4 = (f32[64,256]{1,0:T(8,128)S(1)}, f32[64,256]{1,0:T(8,128)S(1)}) fusion(f32[64,128,256]{2,1,0:T(8,128)S(1)} %get-tuple-element.349, f32[64,128,256]{2,1,0:T(8,128)S(1)} %get-tuple-element.350, f32[128,256]{1,0:T(8,128)S(1)} %get-tuple-element.351, f32[64,128]{1,0:T(8,128)S(1)} %get-tuple-element.352, ...), kind=kLoop, calls=%fused_computation.4.clone.1 | loop fusion | flops 58687488 | bytes 17826048 | tf_op jit(solution)/shard_map/while/body/eval_jaxpr/reduce_sum | solution.py:73
  167.2 0.6 copy-done.4
  168.5 0.5 fusion.41
  169.5 0.5 fusion.42
  171.5 1.8 copy-done.1
  173.2 0.7 copy-done.2
  173.9 3.5 %constant_dynamic-update-slice_fusion.42 = (f32[64,128,256]{2,1,0:T(8,128)S(1)}, f32[16,128,256]{2,1,0:T(8,128)S(1)}, f32[32,128,256]{2,1,0:T(8,128)}, f32[16,128,256]{2,1,0:T(8,128)S(1)}) fusion(f32[64,128,256]{2,1,0:T(8,128)S(1)} %get-tuple-element.325, f32[16,128,256]{2,1,0:T(8,128)} %copy-done.2, f32[128,256]{1,0:T(8,128)S(1)} %slice_bitcast_fusion.32, ...), kind=kLoop, calls=%fused_computation.74.clone.1 | loop fusion | flops 3145728 | bytes 12845056 | tf_op jit(solution)/shard_map/while
  177.8 0.7 slice_bitcast_fusion.34
  178.5 0.7 slice_bitcast_fusion.35
  179.2 4.2 %subtract_dynamic-update-slice_fusion.2 = (f32[64,128,256]{2,1,0:T(8,128)S(1)}, f32[64,128,256]{2,1,0:T(8,128)S(1)}) fusion(f32[64,128,256]{2,1,0:T(8,128)S(1)} %get-tuple-element.343, f32[32,128,256]{2,1,0:T(8,128)} %get-tuple-element.344, f32[32,128,256]{2,1,0:T(8,128)S(1)} %constant_dynamic-update-slice_fusion.43, ...), kind=kLoop, calls=%fused_computation.10.clone.1 | loop fusion | flops 6291456 | bytes 17039360 | tf_op jit(solution)/shard_map/while/body/eval_jaxpr/concatenate | solution.py:46
  183.5 1.0 constant_dynamic-slice_fusion.5
  184.5 10.6 %multiply_reduce_fusion.4 = (f32[64,256]{1,0:T(8,128)S(1)}, f32[64,256]{1,0:T(8,128)S(1)}) fusion(f32[64,128,256]{2,1,0:T(8,128)S(1)} %get-tuple-element.349, f32[64,128,256]{2,1,0:T(8,128)S(1)} %get-tuple-element.350, f32[128,256]{1,0:T(8,128)S(1)} %get-tuple-element.351, f32[64,128]{1,0:T(8,128)S(1)} %get-tuple-element.352, ...), kind=kLoop, calls=%fused_computation.4.clone.1 | loop fusion | flops 58687488 | bytes 17826048 | tf_op jit(solution)/shard_map/while/body/eval_jaxpr/reduce_sum | solution.py:73
  195.1 0.6 copy-done.4
  196.4 0.5 fusion.41
  197.0 0.5 fusion.43
  197.5 0.5 fusion.42
  199.4 1.8 copy-done.1
  201.2 0.7 copy-done.2
  201.9 3.5 %constant_dynamic-update-slice_fusion.42 = (f32[64,128,256]{2,1,0:T(8,128)S(1)}, f32[16,128,256]{2,1,0:T(8,128)S(1)}, f32[32,128,256]{2,1,0:T(8,128)}, f32[16,128,256]{2,1,0:T(8,128)S(1)}) fusion(f32[64,128,256]{2,1,0:T(8,128)S(1)} %get-tuple-element.325, f32[16,128,256]{2,1,0:T(8,128)} %copy-done.2, f32[128,256]{1,0:T(8,128)S(1)} %slice_bitcast_fusion.32, ...), kind=kLoop, calls=%fused_computation.74.clone.1 | loop fusion | flops 3145728 | bytes 12845056 | tf_op jit(solution)/shard_map/while
  205.8 0.7 slice_bitcast_fusion.34
  206.4 0.7 slice_bitcast_fusion.35
  207.1 4.2 %subtract_dynamic-update-slice_fusion.2 = (f32[64,128,256]{2,1,0:T(8,128)S(1)}, f32[64,128,256]{2,1,0:T(8,128)S(1)}) fusion(f32[64,128,256]{2,1,0:T(8,128)S(1)} %get-tuple-element.343, f32[32,128,256]{2,1,0:T(8,128)} %get-tuple-element.344, f32[32,128,256]{2,1,0:T(8,128)S(1)} %constant_dynamic-update-slice_fusion.43, ...), kind=kLoop, calls=%fused_computation.10.clone.1 | loop fusion | flops 6291456 | bytes 17039360 | tf_op jit(solution)/shard_map/while/body/eval_jaxpr/concatenate | solution.py:46
  211.4 1.0 constant_dynamic-slice_fusion.5
  212.4 10.6 %multiply_reduce_fusion.4 = (f32[64,256]{1,0:T(8,128)S(1)}, f32[64,256]{1,0:T(8,128)S(1)}) fusion(f32[64,128,256]{2,1,0:T(8,128)S(1)} %get-tuple-element.349, f32[64,128,256]{2,1,0:T(8,128)S(1)} %get-tuple-element.350, f32[128,256]{1,0:T(8,128)S(1)} %get-tuple-element.351, f32[64,128]{1,0:T(8,128)S(1)} %get-tuple-element.352, ...), kind=kLoop, calls=%fused_computation.4.clone.1 | loop fusion | flops 58687488 | bytes 17826048 | tf_op jit(solution)/shard_map/while/body/eval_jaxpr/reduce_sum | solution.py:73
  223.1 0.6 copy-done.4
  223.8 62.7 %reduce-scatter.2.cloned.1.call-done = f32[16,256]{1,0:T(8,128)} async-done(((f32[128,256]{1,0:T(8,128)}), f32[16,256]{1,0:T(8,128)}) %reduce-scatter.2.cloned.1.call-update) | async-done | bytes 16400 | tf_op jit(solution)/shard_map/reduce_scatter | solution.py:133
  (151 shorter events, 12.6 us)
Async XLA Ops:
  6.5 27.2 %copy-start = (bf16[128,4,1280]{2,1,0:T(4,128)(2,1)S(1)}, bf16[128,4,1280]{2,1,0:T(4,128)(2,1)}, u32[]{:S(2)}) copy-start(bf16[128,4,1280]{2,1,0:T(4,128)(2,1)} %param.9) | copy-start | bytes 3932164
  36.1 5.8 %copy-start.7 = (s32[128,1]{0,1:T(1,128)S(1)}, s32[128,1]{0,1:T(1,128)}, u32[]{:S(2)}) copy-start(s32[128,1]{0,1:T(1,128)} %param.11) | copy-start | bytes 1540
  38.2 47.8 %all-to-all-start.1 = ((bf16[8,24,4,1280]{3,2,1,0:T(4,128)(2,1)}), bf16[8,24,4,1280]{3,2,1,0:T(4,128)(2,1)S(1)}, u32[]{:S(2)}, u32[]{:S(2)}) async-start(bf16[8,24,4,1280]{3,2,1,0:T(4,128)(2,1)} %broadcast_select_fusion), calls=%async_computation.1 | async-start | bytes 3932160 | tf_op jit(solution)/shard_map/all_to_all | solution.py:119
  41.8 70.1 %all-gather.2.cloned.1.call-start = ((), (), s32[]{:S(2)}) async-start(), calls=%async_computation.3 | async-start | bytes 1310720 | tf_op jit(solution)/shard_map/all_gather | solution.py:129
  90.7 3.6 %copy-start.6 = (f32[3,128]{1,0:T(4,128)S(1)}, f32[3,128]{1,0:T(4,128)}, u32[]{:S(2)}) copy-start(f32[3,128]{1,0:T(4,128)} %param.13) | copy-start | bytes 4612
  92.0 4.0 %copy-start.8 = (f32[3,128]{1,0:T(4,128)S(1)}, f32[3,128]{1,0:T(4,128)}, u32[]{:S(2)}) copy-start(f32[3,128]{1,0:T(4,128)} %param.14) | copy-start | bytes 4612
  92.0 20.0 %copy-start.5 = (f32[3,256]{1,0:T(4,128)S(1)}, f32[3,256]{1,0:T(4,128)}, u32[]{:S(2)}) copy-start(f32[3,256]{1,0:T(4,128)} %param.15) | copy-start | bytes 9220
  96.0 190.5 %reduce-scatter.2.cloned.1.call-start = ((), (), s32[]{:S(2)}) async-start(), calls=%async_computation.4 | async-start | bytes 147456 | tf_op jit(solution)/shard_map/reduce_scatter | solution.py:133
  115.4 2.0 copy-start.1
  115.5 2.5 copy-start.2
  128.6 10.6 %copy-start.3 = (f32[128,256]{1,0:T(8,128)S(1)}, f32[128,256]{1,0:T(8,128)}, u32[]{:S(2)}) copy-start(f32[128,256]{1,0:T(8,128)} %get-tuple-element.376) | copy-start | bytes 393220 | tf_op jit(solution)/shard_map/while
  139.2 0.7 copy-start.4
  143.3 2.0 copy-start.1
  143.5 2.5 copy-start.2
  156.6 10.6 %copy-start.3 = (f32[128,256]{1,0:T(8,128)S(1)}, f32[128,256]{1,0:T(8,128)}, u32[]{:S(2)}) copy-start(f32[128,256]{1,0:T(8,128)} %get-tuple-element.376) | copy-start | bytes 393220 | tf_op jit(solution)/shard_map/while
  167.2 0.7 copy-start.4
  171.2 2.0 copy-start.1
  171.4 2.5 copy-start.2
  184.5 10.6 %copy-start.3 = (f32[128,256]{1,0:T(8,128)S(1)}, f32[128,256]{1,0:T(8,128)}, u32[]{:S(2)}) copy-start(f32[128,256]{1,0:T(8,128)} %get-tuple-element.376) | copy-start | bytes 393220 | tf_op jit(solution)/shard_map/while
  195.1 0.7 copy-start.4
  199.2 2.0 copy-start.1
  199.3 2.5 copy-start.2
  212.4 10.6 %copy-start.3 = (f32[128,256]{1,0:T(8,128)S(1)}, f32[128,256]{1,0:T(8,128)}, u32[]{:S(2)}) copy-start(f32[128,256]{1,0:T(8,128)} %get-tuple-element.376) | copy-start | bytes 393220 | tf_op jit(solution)/shard_map/while
  223.1 0.7 copy-start.4
Sparse Core Ops, SparseCore 0:
  96.1 15.8 all-gather.1
  223.9 62.5 reduce-scatter.1
where the time goes:
time: 294 us; the launch traced here: 293 us
  waiting for transfers between devices  117 us (40%)
  other arithmetic  92.2 us (31%)
  local copies, waits for them, and re-layouts  43.5 us (15%)
  blocking collectives  19 us (6%)
  between operations  13.6 us (5%)
  starting transfers between devices  3.68 us (1%)
  matrix products  3.21 us (1%)
    reduce_scatter x1, waiting for transfers between devices, body(): lax.psum_scatter(partial_sum, 'panel', scatter_dimension=0, tiled=True)  62.7 us
    all_to_all x1, waiting for transfers between devices, body(): lax.all_to_all(found, 'panel', split_axis=0, concat_axis=0, tiled=True)  43.7 us
    reduce_sum x4, other arithmetic, radiate(): real_part = jnp.sum((amp_re * cosines + amp_im * sines) * spreading, axis=1)  42.2 us
    while x36, other arithmetic  22.7 us
    concatenate x4, other arithmetic, doubled(): jnp.concatenate([cosines, cosines * last_cos - sines * last_sin], axis=0)  16.6 us
    while x44, local copies, waits for them, and re-layouts  14.6 us
    all_to_all x1, blocking collectives, body(): lax.all_to_all(requests, 'panel', split_axis=0, concat_axis=0, tiled=True)  13.6 us
    scatter x1, local copies, waits for them, and re-layouts, body(): jnp.zeros((peer_count, capacity), jnp.int32).at[owner_of, slot_rank]  11 us
  transfers between devices with their start and end apart: 3, of which 3 were waited for; matrix products, arithmetic and copies ran while one was open for 0% of the time, Pallas kernels for 0%

commit v1 on v0

v1 whole, which is shorter than its diff:
```python
import math

import jax
import jax.numpy as jnp
from jax import lax
from jax.experimental import pallas as pl
from jax.experimental.pallas import tpu as pltpu
from jax.sharding import PartitionSpec as P

NV = 5
NT = 256
HARM = 64


KAPPA = 0.5


def fourier_table(samples, orders):
    sample_ids = jnp.arange(samples, dtype=jnp.int32)
    harmonic = jnp.arange(1, orders + 1, dtype=jnp.int32)
    wrapped = sample_ids[:, None] * harmonic[None, :] % samples
    angles = wrapped.astype(jnp.float32) * (2.0 * math.pi / samples)
    factor = 2.0 / samples
    return jnp.concatenate([factor * jnp.cos(angles), -factor * jnp.sin(angles)], axis=1)


def spectra_of(values, normals, transform, samples):
    panels = values.shape[0]
    fields = values.reshape(panels, NV, samples)
    density = 1.0 + fields[:, 0]
    velocity = fields[:, 1:4]
    pressure_pert = fields[:, 4]
    normal_vec = jnp.transpose(normals)[:, :, None]
    normal_flow = jnp.sum(velocity * normal_vec, axis=1)
    mass_flux = density * normal_flow
    loading = pressure_pert[:, None, :] * normal_vec + mass_flux[:, None, :] * velocity
    series = jnp.concatenate([mass_flux[:, None, :], loading], axis=1)
    return jnp.einsum("pct,tk->cpk", series, transform, precision=lax.Precision.HIGHEST)


GROUP = 8
SLOT = 8


def sin_cos(angle):
    turns = jnp.floor(angle * (2.0 / math.pi) + 0.5)
    reduced = angle - turns * 1.5703125
    reduced = reduced - turns * 4.837512969970703125e-4
    reduced = reduced - turns * 7.54978995489188216e-8
    square = reduced * reduced
    sine = ((-1.9515295891e-4 * square + 8.3321608736e-3) * square - 1.6666654611e-1) * square * reduced + reduced
    cosine = ((2.443315711809948e-5 * square - 1.388731625493765e-3) * square + 4.166664568298827e-2) * square * square - 0.5 * square + 1.0
    quadrant = turns.astype(jnp.int32)
    swap = (quadrant & 1) == 1
    out_sin = jnp.where(swap, cosine, sine)
    out_cos = jnp.where(swap, sine, cosine)
    out_sin = jnp.where((quadrant & 2) == 2, -out_sin, out_sin)
    out_cos = jnp.where(((quadrant + 1) & 2) == 2, -out_cos, out_cos)
    return out_sin, out_cos


def split_hi_lo(array):
    high = array.astype(jnp.bfloat16).astype(jnp.float32)
    return high, array - high


def geometry(points, observers, cos_ref, sin_ref):
    offsets = [observers[i : i + 1, :] - points[:, i : i + 1] for i in range(3)]
    squared = offsets[0] * offsets[0] + offsets[1] * offsets[1] + offsets[2] * offsets[2]
    distance = jnp.sqrt(squared)
    inverse = 1.0 / distance
    weight = inverse * (1.0 / (4.0 * math.pi))
    far = [offset * (inverse * weight) for offset in offsets]
    near = [term * inverse for term in far]
    slots = near + far + [weight, jnp.zeros_like(weight)]
    high, low = split_hi_lo(jnp.concatenate(slots, axis=0))
    right = jnp.concatenate([high, high, low, low], axis=0).astype(jnp.bfloat16)
    sine, cosine = sin_cos(KAPPA * distance)
    twice = 2.0 * cosine
    past_cos, past_sin = jnp.ones_like(cosine), jnp.zeros_like(sine)
    for order in range(8):
        cos_ref[order] = cosine
        sin_ref[order] = sine
        cosine, past_cos = twice * cosine - past_cos, cosine
        sine, past_sin = twice * sine - past_sin, sine
    return right


def amplitude(left, right, out_ref):
    lanes = lax.broadcasted_iota(jnp.int32, (1, left.shape[1]), 1) % GROUP
    rows = left.shape[0]
    masked = [left * (lanes == y).astype(jnp.float32).astype(jnp.bfloat16) for y in range(GROUP)]
    stacked = jnp.concatenate(masked, axis=0)
    out_ref[...] = jnp.dot(stacked, right, preferred_element_type=jnp.float32)


def accumulate(amp_ref, cos_ref, sin_ref, acc_ref):
    rows, observers = acc_ref.shape
    orders = rows // 2
    blocks = orders // 8
    for half in range(observers // 128):
        lane = pl.ds(half * 128, 128)
        acc_re = [acc_ref[pl.ds(8 * b, 8), lane] for b in range(blocks)]
        acc_im = [acc_ref[pl.ds(orders + 8 * b, 8), lane] for b in range(blocks)]
        for y in range(GROUP):
            cosine = cos_ref[:, y, lane]
            sine = sin_ref[:, y, lane]
            step_cos = cos_ref[7, pl.ds(y, 1), lane]
            step_sin = sin_ref[7, pl.ds(y, 1), lane]
            twice = 2.0 * step_cos
            past_cos = past_sin = None
            for b in range(blocks):
                amp_re = amp_ref[pl.ds(y * rows + 8 * b, 8), lane]
                amp_im = amp_ref[pl.ds(y * rows + orders + 8 * b, 8), lane]
                acc_re[b] = acc_re[b] + (amp_re * cosine + amp_im * sine)
                acc_im[b] = acc_im[b] + (amp_im * cosine - amp_re * sine)
                if b == 0:
                    next_cos = cosine * step_cos - sine * step_sin
                    next_sin = sine * step_cos + cosine * step_sin
                else:
                    next_cos = twice * cosine - past_cos
                    next_sin = twice * sine - past_sin
                past_cos, past_sin, cosine, sine = cosine, sine, next_cos, next_sin
        for b in range(blocks):
            acc_ref[pl.ds(8 * b, 8), lane] = acc_re[b]
            acc_ref[pl.ds(orders + 8 * b, 8), lane] = acc_im[b]


def radiate_kernel(coef_ref, points_ref, observer_ref, acc_ref, amp_a, amp_b, cos_a, cos_b, sin_a, sin_b):
    pairs = coef_ref.shape[0]
    observers = observer_ref[...]
    acc_ref[...] = jnp.zeros_like(acc_ref)

    def prepare(pair):
        both = coef_ref[pair]
        half = both.shape[1] // 2
        first = lax.broadcasted_iota(jnp.int32, both.shape, 1) < half
        high, low = split_hi_lo(both)
        left_a = jnp.where(first, high, pltpu.roll(low, half, 1)).astype(jnp.bfloat16)
        left_b = jnp.where(first, pltpu.roll(high, half, 1), low).astype(jnp.bfloat16)
        return jnp.concatenate([left_a, left_a], axis=1), jnp.concatenate([left_b, left_b], axis=1)

    def points_at(group):
        return points_ref[pl.ds(pl.multiple_of(group * GROUP, GROUP), GROUP), :]

    left, _ = prepare(0)
    amplitude(left, geometry(points_at(0), observers, cos_a, sin_a), amp_a)

    @pl.loop(0, pairs)
    def _(pair):
        _, left_b = prepare(pair)
        amplitude(left_b, geometry(points_at(2 * pair + 1), observers, cos_b, sin_b), amp_b)
        accumulate(amp_a, cos_a, sin_a, acc_ref)
        after = jnp.minimum(pair + 1, pairs - 1)
        left_a, _ = prepare(after)
        amplitude(left_a, geometry(points_at(2 * after), observers, cos_a, sin_a), amp_a)
        accumulate(amp_b, cos_b, sin_b, acc_ref)


def radiate_all(spectra, points, observers):
    orders = spectra.shape[2] // 2
    panels = spectra.shape[1]
    wavenum = KAPPA * jnp.arange(1, orders + 1, dtype=jnp.float32)
    turned = jnp.concatenate(
        [-wavenum * spectra[:, :, orders:], wavenum * spectra[:, :, :orders]], axis=2
    )
    slots = jnp.concatenate(
        [spectra[1:4], turned[1:4], turned[0:1], jnp.zeros_like(turned[0:1])], axis=0
    )
    pairs = panels // (2 * GROUP)
    coefs = slots.reshape(SLOT, pairs, 2, GROUP, 2 * orders).transpose(1, 2, 0, 3, 4)
    coefs = coefs.reshape(pairs, 2 * SLOT * GROUP, 2 * orders).transpose(0, 2, 1)
    count = observers.shape[1]
    wave = pltpu.VMEM((8, GROUP, count), jnp.float32)
    amp = pltpu.VMEM((GROUP * 2 * orders, count), jnp.float32)
    return pl.pallas_call(
        radiate_kernel,
        out_shape=jax.ShapeDtypeStruct((2 * orders, count), jnp.float32),
        in_specs=[pl.BlockSpec(memory_space=pltpu.VMEM)] * 3,
        out_specs=pl.BlockSpec(memory_space=pltpu.VMEM),
        scratch_shapes=[amp, amp, wave, wave, wave, wave],
        name="radiate",
    )(coefs, points.T, observers)


def body(
    flow_blocks,
    interp_weights,
    donor_owner,
    donor_block,
    panel_normals,
    panel_points,
    observer_points,
):
    peer_count = lax.axis_size("panel")
    tile_count, tile_width, stencil = interp_weights.shape
    cell_count = flow_blocks.shape[1]
    slot_count = stencil // cell_count
    row_count = tile_count * slot_count
    capacity = max(2, (3 * row_count + 2 * peer_count - 1) // (2 * peer_count))
    owner_of = donor_owner[:, 0]
    matches = (owner_of[:, None] == jnp.arange(peer_count, dtype=jnp.int32)[None, :]).astype(
        jnp.int32
    )
    slot_rank = jnp.sum(jnp.cumsum(matches, axis=0) * matches, axis=1) - 1
    requests = jnp.zeros((peer_count, capacity), jnp.int32).at[owner_of, slot_rank].set(donor_block)
    found = jnp.take(
        flow_blocks,
        lax.all_to_all(requests, "panel", split_axis=0, concat_axis=0, tiled=True),
        axis=0,
    )
    arrived = lax.all_to_all(found, "panel", split_axis=0, concat_axis=0, tiled=True)
    history = arrived.shape[-1]
    flat_rows = arrived.reshape(peer_count * capacity, cell_count, history)
    picked = jnp.take(flat_rows, owner_of * capacity + slot_rank, axis=0)
    donors = picked.reshape(tile_count, stencil, history)
    values = jnp.einsum("tpc,tcv->tpv", interp_weights, donors, preferred_element_type=jnp.float32)
    values = values.reshape(tile_count * tile_width, history)
    transform = fourier_table(NT, HARM)
    spectra = spectra_of(values, panel_normals, transform, NT)
    group_spectra, group_points = (
        lax.all_gather(spectra, "obs", axis=1, tiled=True),
        lax.all_gather(panel_points, "obs", axis=1, tiled=True),
    )
    partial_sum = radiate_all(group_spectra, group_points, observer_points)
    pressure = lax.psum_scatter(partial_sum, "panel", scatter_dimension=0, tiled=True)
    return pressure


def solution(mesh):
    return jax.shard_map(
        body,
        mesh=mesh,
        in_specs=(
            P("panel", None, None),
            P(("panel", "obs"), None, None),
            P(("panel", "obs"), None),
            P(("panel", "obs")),
            P(None, ("panel", "obs")),
            P(None, ("panel", "obs")),
            P(None, "obs"),
        ),
        out_specs=P("panel", "obs"),
        check_vma=False,
    )
```

time: 294 us -> 222 us (0.76)
  other arithmetic: 92.2 us -> 8.98 us
  Pallas kernels: 0 us -> 31.8 us
  local copies, waits for them, and re-layouts: 43.5 us -> 24.6 us
    reduce_sum x8 -> x0, other arithmetic: 42.7 us -> none  [the longest x4 42.2 us: radiate(): real_part = jnp.sum((amp_re * cosines + amp_im * sines) * spreading, axis=1)]
    pallas_call x0 -> x1, Pallas kernels: none -> 31.8 us  [radiate_all(): pl.pallas_call(radiate_kernel, out_shape=jax.ShapeDtypeStruct((2 * orders...]
    while x36 -> x0, other arithmetic: 22.7 us -> none
    concatenate x4 -> x2, other arithmetic: 16.6 us -> 0.36 us  [the longest x1 0.3 us: radiate_all(): jnp.concatenate([spectra[1:4], turned[1:4], turned[0:1], jnp.zeros_like(t...]
    while x44 -> x0, local copies, waits for them, and re-layouts: 14.6 us -> none
    mul x36 -> x0, local copies, waits for them, and re-layouts: 5.75 us -> none  [the longest x16 2.82 us: doubled(): sines * last_sin]
    dynamic_slice x8 -> x0, local copies, waits for them, and re-layouts: 3.91 us -> none  [the longest x4 3.9 us: one_block(): lax.dynamic_slice_in_dim(spectra, first_panel, block_size, 1)]
where the time goes in v1:
time: 222 us
  waiting for transfers between devices  116 us (52%)
  Pallas kernels  31.8 us (14%)
  local copies, waits for them, and re-layouts  24.6 us (11%)
  blocking collectives  19.8 us (9%)
  between operations  13.6 us (6%)
  other arithmetic  8.98 us (4%)
  starting transfers between devices  3.81 us (2%)
  matrix products  3.22 us (1%)
    reduce_scatter x1, waiting for transfers between devices, body(): lax.psum_scatter(partial_sum, 'panel', scatter_dimension=0, tiled=True)  62.6 us
    all_to_all x1, waiting for transfers between devices, body(): lax.all_to_all(found, 'panel', split_axis=0, concat_axis=0, tiled=True)  43.7 us
    pallas_call x1, Pallas kernels, radiate_all(): pl.pallas_call(radiate_kernel, out_shape=jax.ShapeDtypeStruct((2 * orders...  31.8 us
    all_to_all x1, blocking collectives, body(): lax.all_to_all(requests, 'panel', split_axis=0, concat_axis=0, tiled=True)  13.6 us
    scatter x1, local copies, waits for them, and re-layouts, body(): jnp.zeros((peer_count, capacity), jnp.int32).at[owner_of, slot_rank]  11 us
    all_gather x1, waiting for transfers between devices, body(): lax.all_gather(spectra, 'obs', axis=1, tiled=True)  9.54 us
    all_gather x1, blocking collectives, body(): lax.all_gather(panel_points, 'obs', axis=1, tiled=True)  6.21 us
  transfers between devices with their start and end apart: 3, of which 3 were waited for; matrix products, arithmetic and copies ran while one was open for 0% of the time, Pallas kernels for 0%

profile of v1, /device:TPU:0, one launch (start us, length us, event | category | flops | bytes accessed | tf_op | source)
XLA Modules:
  0.0 221.9 jit_solution(15318414980412430547)
XLA Ops:
  6.5 0.0 copy-start
  6.5 0.8 fusion.14
  7.4 0.2 reduce_window_sum.11
  7.6 0.8 select_reduce_fusion
  8.4 0.7 fusion.19
  9.1 11.0 %scatter_fusion = s32[8,24]{1,0:T(8,128)S(1)} fusion(s32[8,24]{1,0:T(8,128)S(1)} %broadcast_in_dim.39, s32[128]{0:T(128)S(1)} %fusion.19, s32[128]{0:T(128)} %param.10), kind=kCustom, calls=%fused_computation.2 | custom fusion | bytes 2560 | tf_op jit(solution)/shard_map/scatter | solution.py:206
  20.0 13.6 %all_to_all.20 = s32[8,1,24]{2,1,0:T(1,128)S(1)} all-to-all(s32[8,1,24]{2,1,0:T(1,128)S(1)} %bitcast.52), channel_id=1, replica_groups=mesh['panel'=8,'obs'=4] {'panel'}, dimensions={0} | all-to-all | bytes 1536 | tf_op jit(solution)/shard_map/all_to_all | solution.py:209
  33.6 0.1 reshape.134
  33.8 0.0 copy-done
  33.8 2.3 %gather_fusion = bf16[192,4,1280]{2,1,0:T(4,128)(2,1)S(1)} fusion(bf16[128,4,1280]{2,1,0:T(4,128)(2,1)S(1)} %copy-done, s32[1024]{0:T(1024)S(1)} %pad_clamp_fusion.1), kind=kCustom, calls=%fused_computation | custom fusion | bytes 3932928 | tf_op jit(solution)/shard_map/jit(_take)/gather | solution.py:207
  36.1 2.1 broadcast_select_fusion
  38.2 0.0 copy-start.3
  38.2 3.7 %all-to-all-start.1 = ((bf16[8,24,4,1280]{3,2,1,0:T(4,128)(2,1)}), bf16[8,24,4,1280]{3,2,1,0:T(4,128)(2,1)S(1)}, u32[]{:S(2)}, u32[]{:S(2)}) async-start(bf16[8,24,4,1280]{3,2,1,0:T(4,128)(2,1)} %broadcast_select_fusion), calls=%async_computation.1 | async-start | bytes 3932160 | tf_op jit(solution)/shard_map/all_to_all | solution.py:212
  42.0 0.0 all-gather.2.cloned.1.call-start
  42.0 0.0 copy-done.3
  42.1 0.3 cosine_multiply_fusion
  42.4 43.7 %all-to-all-done.1 = bf16[8,24,4,1280]{3,2,1,0:T(4,128)(2,1)S(1)} async-done(((bf16[8,24,4,1280]{3,2,1,0:T(4,128)(2,1)}), bf16[8,24,4,1280]{3,2,1,0:T(4,128)(2,1)S(1)}, u32[]{:S(2)}, u32[]{:S(2)}) %all-to-all-start.1) | async-done | bytes 1966112 | tf_op jit(solution)/shard_map/all_to_all | solution.py:212
  86.2 2.7 %gather_fusion.1 = bf16[128,4,1280]{2,1,0:T(4,128)(2,1)} fusion(bf16[192,4,1280]{2,1,0:T(4,128)(2,1)S(1)} %bitcast.57, s32[1024]{0:T(1024)S(1)} %pad_clamp_fusion), kind=kCustom, calls=%fused_computation.1 | custom fusion | bytes 2621952 | tf_op jit(solution)/shard_map/jit(_take)/gather | solution.py:215
  88.9 2.0 broadcast_select_fusion.1
  90.9 0.0 copy-start.1
  90.9 1.3 select_n.72
  92.1 0.0 copy-done.1
  92.1 0.0 copy-start.2
  92.1 1.9 fusion.9
  94.1 0.2 copy.29
  94.2 0.0 copy-start.4
  94.3 0.1 copy.28
  94.4 0.1 copy.23
  94.5 0.0 copy-done.2
  94.5 0.1 multiply_reduce_fusion
  94.6 0.1 multiply_add_fusion
  94.7 1.3 convolution_bitcast_fusion
  96.1 0.0 all-gather.2.cloned.1.call-update
  96.1 0.0 reduce-scatter.2.cloned.1.call-start
  96.2 0.0 copy-done.4
  96.2 0.1 copy.27
  96.3 0.1 pad.3.clone
  96.4 6.2 %all_gather.7 = f32[3,512]{0,1:T(8,128)} all-gather(f32[3,128]{0,1:T(8,128)S(1)} %copy.27), channel_id=1, replica_groups=mesh['panel'=8,'obs'=4] {'obs'}, dimensions={1}, use_global_device_ids=true | all-gather | bytes 7680 | tf_op jit(solution)/shard_map/all_gather | solution.py:223
  102.6 9.5 %all-gather.2.cloned.1.call-done = f32[4,512,128]{1,2,0:T(8,128)} async-done(((f32[4,128,128]{1,2,0:T(8,128)}), f32[4,512,128]{1,2,0:T(8,128)}) %all-gather.2.cloned.1.call-update) | async-done | bytes 1048592 | tf_op jit(solution)/shard_map/all_gather | solution.py:222
  112.1 1.3 slice_multiply_fusion.1
  113.5 0.0 slice-start
  113.5 0.1 fusion.3
  113.5 1.1 slice-done
  114.6 0.3 fusion.1
  114.9 1.9 copy.24
  116.8 1.9 copy.25
  118.6 1.9 copy.26
  120.5 31.8 %radiate.1 = f32[128,256]{1,0:T(8,128)} custom-call(f32[32,128,128]{2,1,0:T(8,128)} %bitcast.53, f32[512,3]{1,0:T(8,128)} %bitcast.61, f32[3,256]{1,0:T(4,128)} %observer_ref.1), custom_call_target="tpu_custom_call" | custom-call | tf_op jit(solution)/shard_map/radiate/pallas_call | solution.py:176
  152.4 0.0 reduce-scatter.2.cloned.1.call-update
  152.4 62.6 %reduce-scatter.2.cloned.1.call-done = f32[16,256]{1,0:T(8,128)} async-done(((f32[128,256]{1,0:T(8,128)}), f32[16,256]{1,0:T(8,128)}) %reduce-scatter.2.cloned.1.call-update) | async-done | bytes 16400 | tf_op jit(solution)/shard_map/reduce_scatter | solution.py:226
  (11 shorter events, 0.1 us)
Async XLA Ops:
  6.5 27.2 %copy-start = (bf16[128,4,1280]{2,1,0:T(4,128)(2,1)S(1)}, bf16[128,4,1280]{2,1,0:T(4,128)(2,1)}, u32[]{:S(2)}) copy-start(bf16[128,4,1280]{2,1,0:T(4,128)(2,1)} %param.7) | copy-start | bytes 3932164
  38.2 3.8 %copy-start.3 = (s32[128,1]{0,1:T(1,128)S(1)}, s32[128,1]{0,1:T(1,128)}, u32[]{:S(2)}) copy-start(s32[128,1]{0,1:T(1,128)} %param.9) | copy-start | bytes 1540
  38.2 47.9 %all-to-all-start.1 = ((bf16[8,24,4,1280]{3,2,1,0:T(4,128)(2,1)}), bf16[8,24,4,1280]{3,2,1,0:T(4,128)(2,1)S(1)}, u32[]{:S(2)}, u32[]{:S(2)}) async-start(bf16[8,24,4,1280]{3,2,1,0:T(4,128)(2,1)} %broadcast_select_fusion), calls=%async_computation.1 | async-start | bytes 3932160 | tf_op jit(solution)/shard_map/all_to_all | solution.py:212
  42.0 70.2 %all-gather.2.cloned.1.call-start = ((), (), s32[]{:S(2)}) async-start(), calls=%async_computation.3 | async-start | bytes 1310720 | tf_op jit(solution)/shard_map/all_gather | solution.py:222
  90.9 1.3 copy-start.1
  92.1 2.3 %copy-start.2 = (f32[3,128]{1,0:T(4,128)S(1)}, f32[3,128]{1,0:T(4,128)}, u32[]{:S(2)}) copy-start(f32[3,128]{1,0:T(4,128)} %param.11) | copy-start | bytes 4612
  94.2 1.9 copy-start.4
  96.1 118.9 %reduce-scatter.2.cloned.1.call-start = ((), (), s32[]{:S(2)}) async-start(), calls=%async_computation.4 | async-start | bytes 147456 | tf_op jit(solution)/shard_map/reduce_scatter | solution.py:226
  113.5 1.1 slice-start
Sparse Core Ops, SparseCore 0:
  96.2 15.8 all-gather.1
  152.5 62.4 reduce-scatter.1

commit v2 on v1

--- a/solution.py
+++ b/solution.py
@@ -1,3 +1,4 @@
+import functools
 import math
 
 import jax
@@ -183,6 +184,60 @@
     )(coefs, points.T, observers)
 
 
+def swap_kernel(axis, spread, source_ref, out_ref, send_sem, recv_sem, local_sem):
+    peers = out_ref.shape[0]
+    me = lax.axis_index(axis)
+    barrier = pltpu.get_barrier_semaphore()
+    for shift in range(1, peers):
+        pl.semaphore_signal(
+            barrier,
+            inc=1,
+            device_id={axis: lax.rem(me + shift, peers)},
+            device_id_type=pl.DeviceIdType.MESH,
+        )
+    own = pltpu.make_async_copy(source_ref.at[me] if spread else source_ref, out_ref.at[me], local_sem)
+    own.start()
+    pl.semaphore_wait(barrier, peers - 1)
+    copies = []
+    for shift in range(1, peers):
+        target = lax.rem(me + shift, peers)
+        copy = pltpu.make_async_remote_copy(
+            src_ref=source_ref.at[target] if spread else source_ref,
+            dst_ref=out_ref.at[me],
+            send_sem=send_sem.at[shift],
+            recv_sem=recv_sem.at[shift],
+            device_id={axis: target},
+            device_id_type=pl.DeviceIdType.MESH,
+        )
+        copy.start()
+        copies.append(copy)
+    own.wait()
+    for copy in copies:
+        copy.wait()
+
+
+def swap(array, axis, spread, number):
+    peers = lax.axis_size(axis)
+    shape = array.shape if spread else (peers,) + array.shape
+    return pl.pallas_call(
+        functools.partial(swap_kernel, axis, spread),
+        out_shape=jax.ShapeDtypeStruct(shape, array.dtype),
+        in_specs=[pl.BlockSpec(memory_space=pltpu.VMEM)],
+        out_specs=pl.BlockSpec(memory_space=pltpu.VMEM),
+        scratch_shapes=[
+            pltpu.SemaphoreType.DMA((peers,)),
+            pltpu.SemaphoreType.DMA((peers,)),
+            pltpu.SemaphoreType.DMA,
+        ],
+        compiler_params=pltpu.CompilerParams(collective_id=number, has_side_effects=True),
+        name=f"swap{number}",
+    )(array)
+
+
+def hot(condition):
+    return condition.astype(jnp.bfloat16)
+
+
 def body(
     flow_blocks,
     interp_weights,
@@ -193,38 +248,52 @@
     observer_points,
 ):
     peer_count = lax.axis_size("panel")
+    me = lax.axis_index("panel")
     tile_count, tile_width, stencil = interp_weights.shape
-    cell_count = flow_blocks.shape[1]
+    held_count, cell_count, history = flow_blocks.shape
     slot_count = stencil // cell_count
     row_count = tile_count * slot_count
     capacity = max(2, (3 * row_count + 2 * peer_count - 1) // (2 * peer_count))
     owner_of = donor_owner[:, 0]
-    matches = (owner_of[:, None] == jnp.arange(peer_count, dtype=jnp.int32)[None, :]).astype(
-        jnp.int32
-    )
-    slot_rank = jnp.sum(jnp.cumsum(matches, axis=0) * matches, axis=1) - 1
-    requests = jnp.zeros((peer_count, capacity), jnp.int32).at[owner_of, slot_rank].set(donor_block)
-    found = jnp.take(
-        flow_blocks,
-        lax.all_to_all(requests, "panel", split_axis=0, concat_axis=0, tiled=True),
-        axis=0,
-    )
-    arrived = lax.all_to_all(found, "panel", split_axis=0, concat_axis=0, tiled=True)
-    history = arrived.shape[-1]
-    flat_rows = arrived.reshape(peer_count * capacity, cell_count, history)
-    picked = jnp.take(flat_rows, owner_of * capacity + slot_rank, axis=0)
-    donors = picked.reshape(tile_count, stencil, history)
-    values = jnp.einsum("tpc,tcv->tpv", interp_weights, donors, preferred_element_type=jnp.float32)
+    wanted = swap(jnp.stack([owner_of, donor_block]), "panel", False, 1)
+    rows = jnp.arange(row_count, dtype=jnp.int32)
+    upto = hot(rows[:, None] <= rows[None, :])
+    asked = wanted[:, 0] == me
+    rank = jnp.dot(hot(asked), upto, preferred_element_type=jnp.float32).astype(jnp.int32) - 1
+    place = jnp.arange(capacity, dtype=jnp.int32)
+    chosen = hot(asked[:, None, :] & (rank[:, None, :] == place[None, :, None]))
+    named = hot(wanted[:, 1][:, :, None] == jnp.arange(held_count, dtype=jnp.int32)[None, None, :])
+    select = jnp.einsum("qsr,qrb->qsb", chosen, named, preferred_element_type=jnp.float32)
+    select = select.astype(jnp.bfloat16).reshape(peer_count * capacity, held_count)
+    flat = flow_blocks.reshape(held_count, cell_count * history)
+    found = jnp.dot(select, flat, preferred_element_type=jnp.float32).astype(jnp.bfloat16)
+    arrived = swap(found.reshape(peer_count, capacity, -1), "panel", True, 2)
+    arrived = arrived.reshape(peer_count * capacity, -1)
+    matches = owner_of[:, None] == jnp.arange(peer_count, dtype=jnp.int32)[None, :]
+    counts = jnp.dot(upto.T, hot(matches), preferred_element_type=jnp.float32)
+    own_rank = jnp.sum(jnp.where(matches, counts, 0.0), axis=1).astype(jnp.int32) - 1
+    target = jnp.repeat(owner_of * capacity + own_rank, cell_count).reshape(tile_count, stencil)
+    lines = jnp.arange(peer_count * capacity, dtype=jnp.int32)
+    cell_of = jnp.arange(stencil, dtype=jnp.int32) % cell_count
+    values = 0.0
+    for cell in range(cell_count):
+        moved = hot((target[:, :, None] == lines) & (cell_of == cell)[None, :, None])
+        weights = jnp.einsum("tpj,tjk->tpk", interp_weights, moved, preferred_element_type=jnp.float32)
+        values = values + jnp.einsum(
+            "tpk,kv->tpv",
+            weights.astype(jnp.bfloat16),
+            arrived[:, cell * history : (cell + 1) * history],
+            preferred_element_type=jnp.float32,
+        )
     values = values.reshape(tile_count * tile_width, history)
     transform = fourier_table(NT, HARM)
     spectra = spectra_of(values, panel_normals, transform, NT)
-    group_spectra, group_points = (
-        lax.all_gather(spectra, "obs", axis=1, tiled=True),
-        lax.all_gather(panel_points, "obs", axis=1, tiled=True),
-    )
-    partial_sum = radiate_all(group_spectra, group_points, observer_points)
-    pressure = lax.psum_scatter(partial_sum, "panel", scatter_dimension=0, tiled=True)
-    return pressure
+    padded = jnp.pad(panel_points.T, ((0, 0), (0, spectra.shape[2] - 3)))
+    group = swap(jnp.concatenate([spectra, padded[None]], axis=0), "obs", False, 3)
+    group = group.transpose(1, 0, 2, 3).reshape(5, -1, group.shape[3])
+    partial_sum = radiate_all(group[:4], group[4, :, :3].T, observer_points)
+    terms = swap(partial_sum.reshape(peer_count, -1, partial_sum.shape[1]), "panel", True, 4)
+    return jnp.sum(terms, axis=0)
 
 
 def solution(mesh):

time: 222 us -> 145 us (0.65)
  waiting for transfers between devices: 116 us -> 0 us
  Pallas kernels: 31.8 us -> 118 us
  blocking collectives: 19.8 us -> 0 us
  local copies, waits for them, and re-layouts: 24.6 us -> 9.22 us
  between operations: 13.6 us -> 0.29 us
  matrix products: 3.22 us -> 9.62 us
  starting transfers between devices: 3.81 us -> 0 us
    pallas_call x0 -> x4, Pallas kernels: none -> 85.7 us  [swap(): pl.pallas_call(functools.partial(swap_kernel, axis, spread), out_shape=ja...]
    reduce_scatter x1 -> x0, waiting for transfers between devices: 62.6 us -> none  [body(): lax.psum_scatter(partial_sum, 'panel', scatter_dimension=0, tiled=True)]
    all_to_all x1 -> x0, waiting for transfers between devices: 43.7 us -> none  [body(): lax.all_to_all(found, 'panel', split_axis=0, concat_axis=0, tiled=True)]
    all_to_all x1 -> x0, blocking collectives: 13.6 us -> none  [body(): lax.all_to_all(requests, 'panel', split_axis=0, concat_axis=0, tiled=True)]
    scatter x1 -> x0, local copies, waits for them, and re-layouts: 11 us -> none  [body(): jnp.zeros((peer_count, capacity), jnp.int32).at[owner_of, slot_rank]]
    all_gather x1 -> x0, waiting for transfers between devices: 9.54 us -> none  [body(): lax.all_gather(spectra, 'obs', axis=1, tiled=True)]
    dot_general x1 -> x8, matrix products: 1.87 us -> 9.04 us  [the longest x4 5.77 us: body(): jnp.einsum('tpk,kv->tpv', weights.astype(jnp.bfloat16), arrived[:, cell *...]
    all_gather x1 -> x0, blocking collectives: 6.21 us -> none  [body(): lax.all_gather(panel_points, 'obs', axis=1, tiled=True)]
  transfers between devices with their start and end apart: 3 -> 0, of which waited for: 3 -> 0; matrix products, arithmetic and copies ran while one was open for 0% -> 0% of each run, Pallas kernels for 0% -> 0%
where the time goes in v2:
time: 145 us
  Pallas kernels  118 us (81%)
  matrix products  9.62 us (7%)
  local copies, waits for them, and re-layouts  9.22 us (6%)
  other arithmetic  8.26 us (6%)
    pallas_call x4, Pallas kernels, swap(): pl.pallas_call(functools.partial(swap_kernel, axis, spread), out_shape=ja...  85.7 us
    pallas_call x1, Pallas kernels, radiate_all(): pl.pallas_call(radiate_kernel, out_shape=jax.ShapeDtypeStruct((2 * orders...  31.8 us
    dot_general x4, matrix products, body(): jnp.einsum('tpk,kv->tpv', weights.astype(jnp.bfloat16), arrived[:, cell *...  5.77 us

profile of v2, /device:TPU:0, one launch (start us, length us, event | category | flops | bytes accessed | tf_op | source)
XLA Modules:
  0.0 144.9 jit_solution(13619521916043215246)
XLA Ops:
  0.0 0.0 copy-start
  0.0 0.9 fusion.2
  0.9 0.7 add_add_fusion
  1.5 0.1 pad.8.clone
  1.6 0.6 fusion.68
  2.2 0.6 fusion.67
  2.8 0.6 fusion.66
  3.4 1.2 pad_add_fusion.source_ref
  4.6 9.6 %swap1.1 = s32[8,2,128]{2,1,0:T(2,128)} custom-call(s32[2,128]{1,0:T(2,128)} %pad_add_fusion.source_ref), custom_call_target="tpu_custom_call" | custom-call | tf_op jit(solution)/shard_map/swap1/pallas_call | solution.py:222
  14.2 0.7 slice_compare_fusion
  14.9 0.7 slice.54
  15.6 0.1 fusion.1
  15.8 0.3 convolution_convert_fusion.4
  16.1 0.1 broadcast_in_dim.11
  16.2 0.1 eq.180
  16.3 0.8 copy.18
  17.1 0.6 pad_bitcast_fusion
  17.7 0.3 cosine_multiply_fusion
  18.1 1.5 %copy.28 = bf16[16,8,4,1280]{3,1,2,0:T(8,128)(2,1)S(1)} copy(bf16[16,8,4,1280]{3,2,1,0:T(4,128)(2,1)} %bitcast.91) | data formatting | bytes 2621440
  19.6 1.9 %convolution_convert_fusion = bf16[192,5120]{1,0:T(8,128)(2,1)} fusion(bf16[192,128]{1,0:T(8,128)(2,1)S(1)} %bitcast.96, bf16[128,5120]{1,0:T(8,128)(2,1)S(1)} %bitcast.85), kind=kOutput, calls=%fused_computation | convolution fusion | flops 252641280 | bytes 3325952 | tf_op jit(solution)/shard_map/dot_general | solution.py:269
  21.5 37.6 %swap2.1 = bf16[8,24,5120]{2,1,0:T(8,128)(2,1)} custom-call(bf16[8,24,5120]{2,1,0:T(8,128)(2,1)} %bitcast.80), custom_call_target="tpu_custom_call" | custom-call | tf_op jit(solution)/shard_map/swap2/pallas_call | solution.py:222
  59.1 0.0 copy-start.2
  59.1 0.0 copy-done
  59.1 1.7 %fusion = f32[128,1280]{1,0:T(8,128)S(1)} fusion(bf16[192,5120]{1,0:T(8,128)(2,1)} %bitcast.81, s32[512]{0:T(512)S(1)} %eq.180, pred[512]{0:T(512)(128)(4,1)S(1)} %fusion.69, bf16[1,128,512]{2,1,0:T(8,128)(2,1)S(1)} %copy-done), kind=kOutput, calls=%fused_computation.11 | convolution fusion | flops 88301568 | bytes 1280512 | tf_op jit(solution)/shard_map/tpk,kv->tpv/dot_general | solution.py:282
  60.8 1.6 %convolution_add_fusion.2 = f32[128,1280]{1,0:T(8,128)S(1)} fusion(f32[128,1280]{1,0:T(8,128)S(1)} %fusion, bf16[192,5120]{1,0:T(8,128)(2,1)} %bitcast.82, s32[512]{0:T(512)S(1)} %eq.180, pred[512]{0:T(512)(128)(4,1)} %fusion.68, bf16[1,128,512]{2,1,0:T(8,128)(2,1)S(1)} %copy-done), kind=kOutput, calls=%fused_computation.3 | convolution fusion | flops 88465408 | bytes 1935872 | tf_op jit(solution)/shard_map/tpk,kv->tpv/dot_general | solution.py:282
  62.4 0.0 copy-done.2
  62.4 1.2 convolution_add_fusion.1
  63.7 1.2 convolution_add_fusion
  64.9 0.0 copy-start.4
  64.9 0.2 copy.13
  65.2 0.0 copy-start.3
  65.2 0.2 copy.27
  65.4 0.1 copy.16
  65.5 0.1 copy.26
  65.6 0.0 copy-done.4
  65.6 0.1 multiply_reduce_fusion
  65.7 0.1 multiply_add_fusion
  65.9 0.6 convolution_bitcast_fusion
  66.5 0.0 copy-done.3
  66.5 0.8 pad_maximum_fusion.source_ref
  67.2 18.2 %swap3.1 = f32[4,5,128,128]{3,2,1,0:T(8,128)} custom-call(f32[5,128,128]{2,1,0:T(8,128)} %pad_maximum_fusion.source_ref), custom_call_target="tpu_custom_call" | custom-call | tf_op jit(solution)/shard_map/swap3/pallas_call | solution.py:222
  85.4 0.0 copy-start.1
  85.4 1.3 slice.77
  86.7 0.1 copy.19
  86.8 0.2 copy-done.1
  87.0 0.1 slice.78
  87.1 0.1 copy.23
  87.2 0.8 slice_bitcast_fusion.points_ref
  87.9 0.1 copy.20
  88.0 0.4 slice_multiply_fusion.1
  88.4 0.1 pad_maximum_fusion.1
  88.5 0.3 fusion.3
  88.8 0.3 maximum_bitcast_fusion
  89.1 0.3 copy.21
  89.4 1.9 %copy.22 = f32[32,128,128]{1,2,0:T(8,128)} copy(f32[32,128,128]{2,1,0:T(8,128)S(1)} %bitcast.79) | data formatting | bytes 4194304 | tf_op jit(solution)/shard_map/reshape | solution.py:173
  91.2 31.8 %radiate.1 = f32[128,256]{1,0:T(8,128)} custom-call(f32[32,128,128]{2,1,0:T(8,128)} %bitcast.78, f32[512,3]{1,0:T(8,128)} %slice_bitcast_fusion.points_ref, f32[3,256]{1,0:T(4,128)} %observer_ref.1), custom_call_target="tpu_custom_call" | custom-call | tf_op jit(solution)/shard_map/radiate/pallas_call | solution.py:177
  123.1 20.3 %swap4.1 = f32[8,16,256]{2,1,0:T(8,128)} custom-call(f32[8,16,256]{2,1,0:T(8,128)} %bitcast.94), custom_call_target="tpu_custom_call" | custom-call | tf_op jit(solution)/shard_map/swap4/pallas_call | solution.py:222
  143.4 1.5 %reduce_sum.32 = f32[16,256]{1,0:T(8,128)} reduce(f32[8,16,256]{2,1,0:T(8,128)} %swap4.1, f32[]{:T(128)} %constant.57.clone.1), dimensions={0}, to_apply=%region_2.3 | reduce | flops 28672 | bytes 147460 | tf_op jit(solution)/shard_map/reduce_sum | solution.py:296
  (7 shorter events, 0.1 us)
Async XLA Ops:
  0.0 59.1 %copy-start = (bf16[1,128,512]{2,1,0:T(8,128)(2,1)S(1)}, bf16[1,128,512]{2,1,0:T(8,128)(2,1)}, u32[]{:S(2)}) copy-start(bf16[1,128,512]{2,1,0:T(8,128)(2,1)} %param.8) | copy-start | bytes 393220
  59.1 3.4 %copy-start.2 = (bf16[8,24,5120]{2,1,0:T(8,128)(2,1)S(1)}, bf16[8,24,5120]{2,1,0:T(8,128)(2,1)}, u32[]{:S(2)}) copy-start(bf16[8,24,5120]{2,1,0:T(8,128)(2,1)} %swap2.1) | copy-start | bytes 5898244
  64.9 0.7 copy-start.4
  65.2 1.3 copy-start.3
  85.4 1.6 %copy-start.1 = (f32[4,5,128,128]{3,2,1,0:T(8,128)S(1)}, f32[4,5,128,128]{3,2,1,0:T(8,128)}, u32[]{:S(2)}) copy-start(f32[4,5,128,128]{3,2,1,0:T(8,128)} %swap3.1) | copy-start | bytes 3932164

commit v3 on v2

--- a/solution.py
+++ b/solution.py
@@ -184,6 +184,14 @@
     )(coefs, points.T, observers)
 
 
+def total_kernel(axis, source_ref, sum_ref, held_ref, send_sem, recv_sem, local_sem):
+    swap_kernel(axis, True, source_ref, held_ref, send_sem, recv_sem, local_sem)
+    total = held_ref[0]
+    for peer in range(1, held_ref.shape[0]):
+        total = total + held_ref[peer]
+    sum_ref[...] = total
+
+
 def swap_kernel(axis, spread, source_ref, out_ref, send_sem, recv_sem, local_sem):
     peers = out_ref.shape[0]
     me = lax.axis_index(axis)
@@ -225,6 +233,24 @@
         in_specs=[pl.BlockSpec(memory_space=pltpu.VMEM)],
         out_specs=pl.BlockSpec(memory_space=pltpu.VMEM),
         scratch_shapes=[
+            pltpu.SemaphoreType.DMA((peers,)),
+            pltpu.SemaphoreType.DMA((peers,)),
+            pltpu.SemaphoreType.DMA,
+        ],
+        compiler_params=pltpu.CompilerParams(collective_id=number, has_side_effects=True),
+        name=f"swap{number}",
+    )(array)
+
+
+def swap_total(array, axis, number):
+    peers = lax.axis_size(axis)
+    return pl.pallas_call(
+        functools.partial(total_kernel, axis),
+        out_shape=jax.ShapeDtypeStruct(array.shape[1:], array.dtype),
+        in_specs=[pl.BlockSpec(memory_space=pltpu.VMEM)],
+        out_specs=pl.BlockSpec(memory_space=pltpu.VMEM),
+        scratch_shapes=[
+            pltpu.VMEM(array.shape, array.dtype),
             pltpu.SemaphoreType.DMA((peers,)),
             pltpu.SemaphoreType.DMA((peers,)),
             pltpu.SemaphoreType.DMA,
@@ -288,12 +314,17 @@
     values = values.reshape(tile_count * tile_width, history)
     transform = fourier_table(NT, HARM)
     spectra = spectra_of(values, panel_normals, transform, NT)
-    padded = jnp.pad(panel_points.T, ((0, 0), (0, spectra.shape[2] - 3)))
-    group = swap(jnp.concatenate([spectra, padded[None]], axis=0), "obs", False, 3)
-    group = group.transpose(1, 0, 2, 3).reshape(5, -1, group.shape[3])
-    partial_sum = radiate_all(group[:4], group[4, :, :3].T, observer_points)
-    terms = swap(partial_sum.reshape(peer_count, -1, partial_sum.shape[1]), "panel", True, 4)
-    return jnp.sum(terms, axis=0)
+    series_count, panels, lanes = spectra.shape
+    padded = jnp.pad(panel_points, ((0, 5), (0, 0))).reshape(-1, lanes)
+    packed = jnp.concatenate([spectra.reshape(-1, lanes), padded], axis=0)
+    group = swap(packed, "obs", False, 3)
+    cut = series_count * panels
+    all_spectra = group[:, :cut].reshape(-1, series_count, panels, lanes).transpose(1, 0, 2, 3)
+    all_spectra = all_spectra.reshape(series_count, -1, lanes)
+    all_points = group[:, cut:].reshape(-1, 8, panels)[:, :3].transpose(1, 0, 2).reshape(3, -1)
+    partial_sum = radiate_all(all_spectra, all_points, observer_points)
+    terms = partial_sum.reshape(peer_count, -1, partial_sum.shape[1])
+    return swap_total(terms, "panel", 4)
 
 
 def solution(mesh):

time: 145 us -> 142 us (0.979)
  Pallas kernels: 118 us -> 115 us
    pallas_call x4 -> x3, Pallas kernels: 85.7 us -> 62.6 us  [swap(): pl.pallas_call(functools.partial(swap_kernel, axis, spread), out_shape=ja...]
    pallas_call x0 -> x1, Pallas kernels: none -> 20.3 us  [swap_total(): pl.pallas_call(functools.partial(total_kernel, axis), out_shape=jax.Shape...]
    transpose x1 -> x2, local copies, waits for them, and re-layouts: 0.11 us -> 1.67 us  [body(): group[:, cut:].reshape(-1, 8, panels)[:, :3].transpose(1, 0, 2)]
    reduce_sum x1 -> x0, other arithmetic: 1.52 us -> none  [body(): return jnp.sum(terms, axis=0)]
where the time goes in v3:
time: 142 us; the launch traced here: 141 us
  Pallas kernels  115 us (81%)
  matrix products  9.58 us (7%)
  local copies, waits for them, and re-layouts  8.96 us (6%)
  other arithmetic  7.43 us (5%)
    pallas_call x3, Pallas kernels, swap(): pl.pallas_call(functools.partial(swap_kernel, axis, spread), out_shape=ja...  62.6 us
    pallas_call x1, Pallas kernels, radiate_all(): pl.pallas_call(radiate_kernel, out_shape=jax.ShapeDtypeStruct((2 * orders...  31.8 us
    pallas_call x1, Pallas kernels, swap_total(): pl.pallas_call(functools.partial(total_kernel, axis), out_shape=jax.Shape...  20.3 us
    dot_general x4, matrix products, body(): jnp.einsum('tpk,kv->tpv', weights.astype(jnp.bfloat16), arrived[:, cell *...  5.68 us
    unnamed x15, local copies, waits for them, and re-layouts  3.27 us

profile of v3, /device:TPU:0, one launch (start us, length us, event | category | flops | bytes accessed | tf_op | source)
XLA Modules:
  0.0 141.0 jit_solution(2554510666385570416)
XLA Ops:
  0.0 0.0 copy-start
  0.0 0.9 fusion.2
  0.9 0.7 add_add_fusion
  1.5 0.1 pad.8.clone
  1.6 0.5 fusion.69
  2.2 0.5 fusion.68
  2.7 0.5 fusion.67
  3.2 1.2 pad_add_fusion.source_ref
  4.5 9.6 %swap1.1 = s32[8,2,128]{2,1,0:T(2,128)} custom-call(s32[2,128]{1,0:T(2,128)} %pad_add_fusion.source_ref), custom_call_target="tpu_custom_call" | custom-call | tf_op jit(solution)/shard_map/swap1/pallas_call | solution.py:230
  14.1 0.7 slice_compare_fusion
  14.8 0.7 slice.52
  15.5 0.1 fusion.1
  15.7 0.3 convolution_convert_fusion.4
  16.0 0.1 broadcast_in_dim.8
  16.1 0.1 eq.180
  16.2 1.2 cosine_multiply_fusion
  17.4 1.5 %copy.22 = bf16[16,8,4,1280]{3,1,2,0:T(8,128)(2,1)S(1)} copy(bf16[16,8,4,1280]{3,2,1,0:T(4,128)(2,1)} %bitcast.93) | data formatting | bytes 2621440
  18.9 1.9 %convolution_convert_fusion = bf16[192,5120]{1,0:T(8,128)(2,1)} fusion(bf16[192,128]{1,0:T(8,128)(2,1)S(1)} %bitcast.99, bf16[128,5120]{1,0:T(8,128)(2,1)S(1)} %bitcast.87), kind=kOutput, calls=%fused_computation | convolution fusion | flops 252641280 | bytes 3325952 | tf_op jit(solution)/shard_map/dot_general | solution.py:295
  20.8 37.6 %swap2.1 = bf16[8,24,5120]{2,1,0:T(8,128)(2,1)} custom-call(bf16[8,24,5120]{2,1,0:T(8,128)(2,1)} %bitcast.82), custom_call_target="tpu_custom_call" | custom-call | tf_op jit(solution)/shard_map/swap2/pallas_call | solution.py:230
  58.4 0.0 copy-start.1
  58.4 0.0 copy-done
  58.4 1.7 %fusion = f32[128,1280]{1,0:T(8,128)S(1)} fusion(bf16[192,5120]{1,0:T(8,128)(2,1)} %bitcast.83, s32[512]{0:T(512)S(1)} %eq.180, pred[512]{0:T(512)(128)(4,1)S(1)} %fusion.70, bf16[1,128,512]{2,1,0:T(8,128)(2,1)S(1)} %copy-done), kind=kOutput, calls=%fused_computation.10 | convolution fusion | flops 88301568 | bytes 1280512 | tf_op jit(solution)/shard_map/tpk,kv->tpv/dot_general | solution.py:308
  60.1 1.6 %convolution_add_fusion.2 = f32[128,1280]{1,0:T(8,128)S(1)} fusion(f32[128,1280]{1,0:T(8,128)S(1)} %fusion, bf16[192,5120]{1,0:T(8,128)(2,1)} %bitcast.84, s32[512]{0:T(512)S(1)} %eq.180, pred[512]{0:T(512)(128)(4,1)} %fusion.69, bf16[1,128,512]{2,1,0:T(8,128)(2,1)S(1)} %copy-done), kind=kOutput, calls=%fused_computation.3 | convolution fusion | flops 88465408 | bytes 1935872 | tf_op jit(solution)/shard_map/tpk,kv->tpv/dot_general | solution.py:308
  61.7 0.0 copy-done.1
  61.7 1.2 convolution_add_fusion.1
  62.9 1.2 convolution_add_fusion
  64.1 0.0 copy-start.3
  64.1 0.2 copy.11
  64.4 0.0 copy-start.2
  64.4 0.2 copy.21
  64.6 0.0 copy-start.4
  64.6 0.1 copy.14
  64.7 0.1 copy.20
  64.8 0.0 copy-done.3
  64.8 0.1 multiply_reduce_fusion
  65.0 0.1 multiply_add_fusion
  65.1 0.2 copy-done.2
  65.3 0.7 fusion.4
  66.0 0.0 copy-done.4
  66.0 0.7 select_maximum_fusion.source_ref
  66.7 15.4 %swap3.1 = f32[4,520,128]{2,1,0:T(8,128)} custom-call(f32[520,128]{1,0:T(8,128)} %select_maximum_fusion.source_ref), custom_call_target="tpu_custom_call" | custom-call | tf_op jit(solution)/shard_map/swap3/pallas_call | solution.py:230
  82.1 0.0 slice-start
  82.1 0.8 slice_bitcast_fusion.1
  82.9 0.4 slice-done
  83.4 0.1 copy.27
  83.4 0.9 copy.18
  84.3 0.1 slice.74
  84.4 0.4 slice_multiply_fusion.1
  84.7 0.1 pad_maximum_fusion
  84.9 0.3 fusion.3
  85.1 0.3 maximum_bitcast_fusion
  85.4 0.3 copy.16
  85.7 1.9 %copy.17 = f32[32,128,128]{1,2,0:T(8,128)} copy(f32[32,128,128]{2,1,0:T(8,128)S(1)} %bitcast.81) | data formatting | bytes 4194304 | tf_op jit(solution)/shard_map/reshape | solution.py:173
  87.5 31.8 %radiate.1 = f32[128,256]{1,0:T(8,128)} custom-call(f32[32,128,128]{2,1,0:T(8,128)} %bitcast.80, f32[512,3]{1,0:T(8,128)} %bitcast.96, f32[3,256]{1,0:T(4,128)} %observer_ref.1), custom_call_target="tpu_custom_call" | custom-call | tf_op jit(solution)/shard_map/radiate/pallas_call | solution.py:177
  119.4 20.3 %swap4.1 = f32[16,256]{1,0:T(8,128)} custom-call(f32[8,16,256]{2,1,0:T(8,128)} %bitcast.98), custom_call_target="tpu_custom_call" | custom-call | tf_op jit(solution)/shard_map/swap4/pallas_call | solution.py:247
  139.7 1.3 copy.29
  (7 shorter events, 0.1 us)
Async XLA Ops:
  0.0 58.4 %copy-start = (bf16[1,128,512]{2,1,0:T(8,128)(2,1)S(1)}, bf16[1,128,512]{2,1,0:T(8,128)(2,1)}, u32[]{:S(2)}) copy-start(bf16[1,128,512]{2,1,0:T(8,128)(2,1)} %param.8) | copy-start | bytes 393220
  58.4 3.4 %copy-start.1 = (bf16[8,24,5120]{2,1,0:T(8,128)(2,1)S(1)}, bf16[8,24,5120]{2,1,0:T(8,128)(2,1)}, u32[]{:S(2)}) copy-start(bf16[8,24,5120]{2,1,0:T(8,128)(2,1)} %swap2.1) | copy-start | bytes 5898244
  64.1 0.7 copy-start.3
  64.4 0.9 copy-start.2
  64.6 1.4 copy-start.4
  82.1 1.2 slice-start
